TPU v7x, 32 devices: a whole 2x2x4 slice. The times are simulated.
32 devices in a mesh: gx: 4 (over x, core), gy: 8 (over z, y).
Axes of the slice: x: 2, y: 2, z: 4, core: 2. Of those that a mesh axis runs over, the one named last changes fastest.
Arguments:
- tokens: bfloat16 [2740, 1024], P('gx', 'gy'), may hold values from -64 to 64
- cotangent: bfloat16 [2740, 1024], P('gx', 'gy'), may hold values from -6 to 6
- norm1_gain: float32 [1024], P('gy'), may hold values from 0.1 to 1.9
- norm1_shift: float32 [1024], P('gy'), may hold values from -1.5 to 1.5
- qkv_weight: bfloat16 [1024, 3072], P('gx', 'gy'), may hold values from -4 to 4
- qv_bias: float32 [2048], P('gy'), may hold values from -2.5 to 2.5
- proj_weight: bfloat16 [1024, 1024], P('gx', 'gy'), may hold values from -1.5 to 1.5
- proj_bias: float32 [1024], P('gy'), may hold values from -1.5 to 1.5
- scale_attn: float32 [1024], P('gy'), may hold values from 0.3 to 1.5
- norm2_gain: float32 [1024], P('gy'), may hold values from 0.1 to 1.9
- norm2_shift: float32 [1024], P('gy'), may hold values from -1.5 to 1.5
- fc1_weight: bfloat16 [1024, 4096], P('gx', 'gy'), may hold values from -0.1875 to 0.1875
- fc1_bias: float32 [4096], P('gy'), may hold values from -2.5 to 2.5
- fc2_weight: bfloat16 [4096, 1024], P('gx', 'gy'), may hold values from -0.09375 to 0.09375
- fc2_bias: float32 [1024], P('gy'), may hold values from -1.5 to 1.5
- scale_mlp: float32 [1024], P('gy'), may hold values from 0.3 to 1.5
Outputs:
- output: float32 [2740, 1024], P('gx', 'gy')
- grad_tokens: float32 [2740, 1024], P('gx', 'gy')
- grad_norm1_gain: float32 [1024], P('gy')
- grad_norm1_shift: float32 [1024], P('gy')
- grad_qkv_weight: float32 [1024, 3072], P('gx', 'gy')
- grad_qv_bias: float32 [2048], P('gy')
- grad_proj_weight: float32 [1024, 1024], P('gx', 'gy')
- grad_proj_bias: float32 [1024], P('gy')
- grad_scale_attn: float32 [1024], P('gy')
- grad_norm2_gain: float32 [1024], P('gy')
- grad_norm2_shift: float32 [1024], P('gy')
- grad_fc1_weight: float32 [1024, 4096], P('gx', 'gy')
- grad_fc1_bias: float32 [4096], P('gy')
- grad_fc2_weight: float32 [4096, 1024], P('gx', 'gy')
- grad_fc2_bias: float32 [1024], P('gy')
- grad_scale_mlp: float32 [1024], P('gy')
All inputs are finite; a program needn't handle non-finite values.
Results may differ from a plain program's by a relative error of at most 0.012.
Values may be sent and summed in bfloat16 or wider, within the bound.
A program may use at most 128 MiB of HBM per device.

v0:
```python
import jax
import jax.numpy as jnp
from jax import lax
from jax.sharding import PartitionSpec as P

D = 1024
HD = 64
IMGS = 1


EPS = 1e-06
ROOT_HALF = 0.7071067811865476
INV_ROOT_TAU = 0.3989422804014327


def from_partner(block, axis, bit):
    count = lax.axis_size(axis)
    route = []
    for low in range(count):
        high = low | 1 << bit
        if high != low and high < count:
            route += [(low, high), (high, low)]
    return lax.ppermute(block, axis, route)


def normal_cdf(values):
    return 0.5 * (1.0 + jax.scipy.special.erf(values * ROOT_HALF))


def gelu_exact(values):
    return values * normal_cdf(values)


def gelu_slope(values):
    return normal_cdf(values) + values * jnp.exp(-0.5 * values * values) * INV_ROOT_TAU


def norm_forward(rows, gain, shift):
    totals, squares = lax.psum((jnp.sum(rows, axis=1), jnp.sum(rows * rows, axis=1)), "gy")
    row_mean = totals / D
    inv_std = lax.rsqrt(squares / D - row_mean * row_mean + EPS)[:, None]
    normed = (rows - row_mean[:, None]) * inv_std
    return (normed, inv_std, (normed * gain + shift).astype(jnp.bfloat16))


def norm_backward(grad_normed, normed, inv_std, gain):
    scaled = grad_normed * gain
    first, second = lax.psum((jnp.sum(scaled, axis=1), jnp.sum(scaled * normed, axis=1)), "gy")
    return inv_std * (scaled - first[:, None] / D - normed * (second[:, None] / D))


def project(inputs, weight):
    result = jnp.dot(
        lax.all_gather(inputs, "gy", axis=1, tiled=True), weight, preferred_element_type=jnp.float32
    )
    return (result, inputs)


def weight_grad(saved, grad_out):
    return jnp.einsum(
        "tk,tn->kn",
        lax.all_gather(saved, "gy", axis=1, tiled=True),
        grad_out,
        preferred_element_type=jnp.float32,
    )


def back_project(grad_out, weight):
    term = jnp.einsum("tn,kn->tk", grad_out, weight, preferred_element_type=jnp.float32)
    return lax.psum_scatter(term, "gy", scatter_dimension=1, tiled=True)


def on_device(
    tokens,
    cotangent,
    norm1_gain,
    norm1_shift,
    qkv_weight,
    qv_bias,
    proj_weight,
    proj_bias,
    scale_attn,
    norm2_gain,
    norm2_shift,
    fc1_weight,
    fc1_bias,
    fc2_weight,
    fc2_bias,
    scale_mlp,
):
    count = tokens.shape[0]
    half_len = count // IMGS
    heads_here = qkv_weight.shape[1] // (3 * HD)
    factor = HD ** (-0.5)
    full_qkv, full_proj, full_fc1, full_fc2 = (
        lax.all_gather(qkv_weight, "gx", axis=0, tiled=True),
        lax.all_gather(proj_weight, "gx", axis=0, tiled=True),
        lax.all_gather(fc1_weight, "gx", axis=0, tiled=True),
        lax.all_gather(fc2_weight, "gx", axis=0, tiled=True),
    )
    inputs = tokens.astype(jnp.float32)
    normed_one, inv_one, norm_one = norm_forward(inputs, norm1_gain, norm1_shift)
    mixed, saved_one = project(norm_one, full_qkv)
    mixed = mixed.reshape(count, heads_here, 3, HD)
    biases = qv_bias.reshape(heads_here, 2, HD)
    queries = (mixed[:, :, 0] + biases[:, 0]).astype(jnp.bfloat16)
    keys = mixed[:, :, 1].astype(jnp.bfloat16)
    values = (mixed[:, :, 2] + biases[:, 1]).astype(jnp.bfloat16)
    lower = lax.axis_index("gx") % 2 == 0
    pair_kv = jnp.concatenate([keys, values], axis=2).reshape(count, heads_here * 2 * HD)
    other_kv = from_partner(pair_kv, "gx", 0)
    first_kv = jnp.where(lower, pair_kv, other_kv)
    second_kv = jnp.where(lower, other_kv, pair_kv)
    image_shape = (IMGS, half_len, heads_here, 2 * HD)
    both_kv = jnp.concatenate(
        [first_kv.reshape(image_shape), second_kv.reshape(image_shape)], axis=1
    )
    key_all = both_kv[..., :HD]
    value_all = both_kv[..., HD:]
    query_img = queries.reshape(IMGS, half_len, heads_here, HD)
    scores = (
        jnp.einsum("iqhe,ikhe->ihqk", query_img, key_all, preferred_element_type=jnp.float32)
        * factor
    )
    row_max = jnp.max(scores, axis=3, keepdims=True)
    exponent = jnp.exp(scores - row_max)
    totals = jnp.sum(exponent, axis=3, keepdims=True)
    log_total = row_max + jnp.log(totals)
    probs = (exponent / totals).astype(jnp.bfloat16)
    attended_img = jnp.einsum(
        "ihqk,ikhe->iqhe", probs, value_all, preferred_element_type=jnp.float32
    ).astype(jnp.bfloat16)
    attended = attended_img.reshape(count, heads_here * HD)
    attn_out, saved_two = project(attended, full_proj)
    attn_out = attn_out + proj_bias
    middle = inputs + scale_attn * attn_out
    normed_two, inv_two, norm_two = norm_forward(middle, norm2_gain, norm2_shift)
    pre_act, saved_three = project(norm_two, full_fc1)
    pre_act = pre_act + fc1_bias
    hidden = gelu_exact(pre_act).astype(jnp.bfloat16)
    mlp_out, saved_four = project(hidden, full_fc2)
    mlp_out = mlp_out + fc2_bias
    output = middle + scale_mlp * mlp_out
    upstream = cotangent.astype(jnp.float32)
    grad_scale_mlp = jnp.sum(upstream * mlp_out, axis=0)
    grad_mlp = upstream * scale_mlp
    grad_fc2_bias = jnp.sum(grad_mlp, axis=0)
    grad_mlp_b = grad_mlp.astype(jnp.bfloat16)
    grad_fc2 = weight_grad(saved_four, grad_mlp_b)
    grad_hidden = back_project(grad_mlp_b, full_fc2)
    grad_pre = grad_hidden * gelu_slope(pre_act)
    grad_fc1_bias = jnp.sum(grad_pre, axis=0)
    grad_pre_b = grad_pre.astype(jnp.bfloat16)
    grad_fc1 = weight_grad(saved_three, grad_pre_b)
    grad_norm_two = back_project(grad_pre_b, full_fc1)
    grad_gain_two = jnp.sum(grad_norm_two * normed_two, axis=0)
    grad_shift_two = jnp.sum(grad_norm_two, axis=0)
    grad_middle = upstream + norm_backward(grad_norm_two, normed_two, inv_two, norm2_gain)
    grad_scale_attn = jnp.sum(grad_middle * attn_out, axis=0)
    grad_attn = grad_middle * scale_attn
    grad_proj_bias = jnp.sum(grad_attn, axis=0)
    grad_attn_b = grad_attn.astype(jnp.bfloat16)
    grad_proj = weight_grad(saved_two, grad_attn_b)
    grad_attended = back_project(grad_attn_b, full_proj).astype(jnp.bfloat16)
    grad_att_img = grad_attended.reshape(IMGS, half_len, heads_here, HD)
    recomputed = jnp.exp(scores - log_total)
    probs_b = recomputed.astype(jnp.bfloat16)
    grad_value_all = jnp.einsum(
        "ihqk,iqhe->ikhe", probs_b, grad_att_img, preferred_element_type=jnp.float32
    )
    grad_probs = jnp.einsum(
        "iqhe,ikhe->ihqk", grad_att_img, value_all, preferred_element_type=jnp.float32
    )
    delta = jnp.sum(grad_att_img.astype(jnp.float32) * attended_img.astype(jnp.float32), axis=3)
    grad_scores = recomputed * (grad_probs - jnp.transpose(delta, (0, 2, 1))[..., None])
    grad_scores_b = grad_scores.astype(jnp.bfloat16)
    grad_query = (
        jnp.einsum("ihqk,ikhe->iqhe", grad_scores_b, key_all, preferred_element_type=jnp.float32)
        * factor
    )
    grad_key_all = (
        jnp.einsum("ihqk,iqhe->ikhe", grad_scores_b, query_img, preferred_element_type=jnp.float32)
        * factor
    )
    grad_kv_all = jnp.concatenate([grad_key_all, grad_value_all], axis=3)
    first_part = grad_kv_all[:, :half_len].reshape(count, heads_here * 2 * HD)
    second_part = grad_kv_all[:, half_len:].reshape(count, heads_here * 2 * HD)
    own_part = jnp.where(lower, first_part, second_part)
    sent_part = jnp.where(lower, second_part, first_part)
    grad_kv = own_part + from_partner(sent_part.astype(jnp.bfloat16), "gx", 0).astype(
        sent_part.dtype
    )
    grad_kv = grad_kv.reshape(count, heads_here, 2, HD)
    grad_query = grad_query.reshape(count, heads_here, HD)
    grad_qv_bias = jnp.stack(
        [jnp.sum(grad_query, axis=0), jnp.sum(grad_kv[:, :, 1], axis=0)], axis=1
    ).reshape(heads_here * 2 * HD)
    grad_mixed = (
        jnp.stack([grad_query, grad_kv[:, :, 0], grad_kv[:, :, 1]], axis=2)
        .astype(jnp.bfloat16)
        .reshape(count, heads_here * 3 * HD)
    )
    grad_qkv = weight_grad(saved_one, grad_mixed)
    grad_norm_one = back_project(grad_mixed, full_qkv)
    grad_gain_one = jnp.sum(grad_norm_one * normed_one, axis=0)
    grad_shift_one = jnp.sum(grad_norm_one, axis=0)
    grad_input = grad_middle + norm_backward(grad_norm_one, normed_one, inv_one, norm1_gain)
    grad_qkv, grad_proj, grad_fc1, grad_fc2 = (
        lax.psum_scatter(
            grad_qkv.astype(jnp.bfloat16), "gx", scatter_dimension=0, tiled=True
        ).astype(jnp.float32),
        lax.psum_scatter(
            grad_proj.astype(jnp.bfloat16), "gx", scatter_dimension=0, tiled=True
        ).astype(jnp.float32),
        lax.psum_scatter(
            grad_fc1.astype(jnp.bfloat16), "gx", scatter_dimension=0, tiled=True
        ).astype(jnp.float32),
        lax.psum_scatter(
            grad_fc2.astype(jnp.bfloat16), "gx", scatter_dimension=0, tiled=True
        ).astype(jnp.float32),
    )
    smalls = lax.psum(
        (
            grad_gain_one,
            grad_shift_one,
            grad_qv_bias,
            grad_proj_bias,
            grad_scale_attn,
            grad_gain_two,
            grad_shift_two,
            grad_fc1_bias,
            grad_fc2_bias,
            grad_scale_mlp,
        ),
        "gx",
    )
    return (
        output,
        grad_input,
        smalls[0],
        smalls[1],
        grad_qkv,
        smalls[2],
        grad_proj,
        smalls[3],
        smalls[4],
        smalls[5],
        smalls[6],
        grad_fc1,
        smalls[7],
        grad_fc2,
        smalls[8],
        smalls[9],
    )


def solution(mesh):
    return jax.shard_map(
        on_device,
        mesh=mesh,
        in_specs=(
            P("gx", "gy"),
            P("gx", "gy"),
            P("gy"),
            P("gy"),
            P("gx", "gy"),
            P("gy"),
            P("gx", "gy"),
            P("gy"),
            P("gy"),
            P("gy"),
            P("gy"),
            P("gx", "gy"),
            P("gy"),
            P("gx", "gy"),
            P("gy"),
            P("gy"),
        ),
        out_specs=(
            P("gx", "gy"),
            P("gx", "gy"),
            P("gy"),
            P("gy"),
            P("gx", "gy"),
            P("gy"),
            P("gx", "gy"),
            P("gy"),
            P("gy"),
            P("gy"),
            P("gy"),
            P("gx", "gy"),
            P("gy"),
            P("gx", "gy"),
            P("gy"),
            P("gy"),
        ),
        check_vma=False,
    )
```

profile of v0, /device:TPU:0, one launch (start us, length us, event | category | flops | bytes accessed | tf_op | source)
XLA Modules:
  0.0 869.4 jit_solution(13419016381353141579)
XLA Ops:
  8.4 23.4 %all-reduce.3 = (f32[685]{0:T(1024)S(1)}, f32[685]{0:T(1024)S(1)}) all-reduce(f32[685]{0:T(1024)S(1)} %get-tuple-element.31, f32[685]{0:T(1024)S(1)} %get-tuple-element.30), channel_id=1, replica_groups=mesh['gx'=4,'gy'=8] {'gy'}, use_global_device_ids=true, to_apply=%region_3.0 | all-reduce | flops 1370 | bytes 10960 | tf_op jit(solution)/shard_map/psum | solution.py:39
  35.1 8.8 %all_gather.29 = bf16[1024,384]{1,0:T(8,128)(2,1)S(1)} all-gather(bf16[256,384]{1,0:T(8,128)(2,1)} %param.20), channel_id=1, replica_groups=mesh['gx'=4,'gy'=8] {'gx'}, dimensions={0}, use_global_device_ids=true | all-gather | bytes 983040 | tf_op jit(solution)/shard_map/all_gather | solution.py:96
  43.9 30.4 %all-gather.7.cloned.1.call-done = bf16[685,1024]{1,0:T(8,128)(2,1)} async-done(((bf16[685,128]{1,0:T(8,128)(2,1)}), bf16[685,1024]{1,0:T(8,128)(2,1)}) %all-gather.7.cloned.1.call-update) | async-done | bytes 1402896 | tf_op jit(solution)/shard_map/all_gather | solution.py:54
  87.4 5.8 all_gather.31
  93.2 35.4 %all-gather.9.cloned.1.call-done = bf16[685,1024]{0,1:T(8,128)(2,1)} async-done(((bf16[685,128]{0,1:T(8,128)(2,1)}), bf16[685,1024]{0,1:T(8,128)(2,1)}) %all-gather.9.cloned.1.call-update) | async-done | bytes 1402896 | tf_op jit(solution)/shard_map/all_gather | solution.py:54
  130.8 19.1 %all-reduce.2 = (f32[685]{0:T(1024)S(1)}, f32[685]{0:T(1024)S(1)}) all-reduce(f32[685]{0:T(1024)S(1)} %get-tuple-element.27, f32[685]{0:T(1024)S(1)} %get-tuple-element.26), channel_id=1, replica_groups=mesh['gx'=4,'gy'=8] {'gy'}, use_global_device_ids=true, to_apply=%region_9.10 | all-reduce | flops 1370 | bytes 10960 | tf_op jit(solution)/shard_map/psum | solution.py:39
  150.9 7.1 fusion.45
  158.1 5.3 all-gather.13.cloned.1.call-done
  163.4 45.1 %all-gather.11.cloned.1.call-done = bf16[685,1024]{1,0:T(8,128)(2,1)} async-done(((bf16[685,128]{1,0:T(8,128)(2,1)}), bf16[685,1024]{1,0:T(8,128)(2,1)}) %all-gather.11.cloned.1.call-update) | async-done | bytes 1402896 | tf_op jit(solution)/shard_map/all_gather | solution.py:54
  208.5 191.3 %reduce-scatter.9.cloned.1.call-done = f32[685,512]{1,0:T(8,128)} async-done(((f32[685,4096]{1,0:T(8,128)}), f32[685,512]{1,0:T(8,128)}) %reduce-scatter.9.cloned.1.call-update) | async-done | bytes 1402896 | tf_op jit(solution)/shard_map/reduce_scatter | solution.py:70
  399.8 5.0 fusion.60
  409.1 72.3 %reduce-scatter.11.cloned.1.call-done = f32[685,128]{1,0:T(8,128)} async-done(((f32[685,1024]{1,0:T(8,128)}), f32[685,128]{1,0:T(8,128)}) %reduce-scatter.11.cloned.1.call-update) | async-done | bytes 350736 | tf_op jit(solution)/shard_map/reduce_scatter | solution.py:70
  483.3 20.7 %all-reduce.1 = (f32[685]{0:T(1024)S(1)}, f32[685]{0:T(1024)S(1)}) all-reduce(f32[685]{0:T(1024)S(1)} %get-tuple-element.17, f32[685]{0:T(1024)S(1)} %get-tuple-element.21), channel_id=1, replica_groups=mesh['gx'=4,'gy'=8] {'gy'}, use_global_device_ids=true, to_apply=%region_15.16 | all-reduce | flops 1370 | bytes 10960 | tf_op jit(solution)/shard_map/psum | solution.py:48
  504.0 70.5 %all-gather.15.cloned.1.call-done = bf16[685,4096]{1,0:T(8,128)(2,1)} async-done(((bf16[685,512]{1,0:T(8,128)(2,1)}), bf16[685,4096]{1,0:T(8,128)(2,1)}) %all-gather.15.cloned.1.call-update) | async-done | bytes 5611536 | tf_op jit(solution)/shard_map/all_gather | solution.py:54
  574.6 5.6 fusion.26
  587.9 5.5 convolution_convert_fusion
  593.5 60.7 %reduce-scatter.13.cloned.1.call-done = f32[685,128]{1,0:T(8,128)} async-done(((f32[685,1024]{1,0:T(8,128)}), f32[685,128]{1,0:T(8,128)}) %reduce-scatter.13.cloned.1.call-update) | async-done | bytes 350736 | tf_op jit(solution)/shard_map/reduce_scatter | solution.py:70
  659.8 6.2 multiply_convert_fusion
  682.3 20.8 %reduce-scatter.19.cloned.1.call-done = bf16[256,128]{1,0:T(8,128)(2,1)} async-done(((bf16[1024,128]{1,0:T(8,128)(2,1)}), bf16[256,128]{1,0:T(8,128)(2,1)}) %reduce-scatter.19.cloned.1.call-update) | async-done | bytes 65552 | tf_op jit(solution)/shard_map/reduce_scatter | solution.py:212
  704.6 25.7 %reduce-scatter.23.cloned.1.call-done = bf16[1024,128]{1,0:T(8,128)(2,1)} async-done(((bf16[4096,128]{1,0:T(8,128)(2,1)}), bf16[1024,128]{1,0:T(8,128)(2,1)}) %reduce-scatter.23.cloned.1.call-update) | async-done | bytes 262160 | tf_op jit(solution)/shard_map/reduce_scatter | solution.py:218
  732.3 23.8 %reduce-scatter.17.cloned.1.call-done = bf16[256,384]{1,0:T(8,128)(2,1)} async-done(((bf16[1024,384]{1,0:T(8,128)(2,1)}), bf16[256,384]{1,0:T(8,128)(2,1)}) %reduce-scatter.17.cloned.1.call-update) | async-done | bytes 196624 | tf_op jit(solution)/shard_map/reduce_scatter | solution.py:209
  757.8 75.2 %reduce-scatter.15.cloned.1.call-done = f32[685,128]{1,0:T(8,128)} async-done(((f32[685,1024]{1,0:T(8,128)}), f32[685,128]{1,0:T(8,128)}) %reduce-scatter.15.cloned.1.call-update) | async-done | bytes 350736 | tf_op jit(solution)/shard_map/reduce_scatter | solution.py:70
  834.5 19.8 %all-reduce = (f32[685]{0:T(1024)S(1)}, f32[685]{0:T(1024)S(1)}) all-reduce(f32[685]{0:T(1024)S(1)} %get-tuple-element.19, f32[685]{0:T(1024)S(1)} %get-tuple-element.20), channel_id=1, replica_groups=mesh['gx'=4,'gy'=8] {'gy'}, use_global_device_ids=true, to_apply=%region_22.23 | all-reduce | flops 1370 | bytes 10960 | tf_op jit(solution)/shard_map/psum | solution.py:48
  854.4 6.3 all-reduce.4
  (175 shorter events, 64.8 us)
Async XLA Ops:
  7.2 67.2 %all-gather.7.cloned.1.call-start = ((), (), s32[]{:S(2)}) async-start(), calls=%async_computation.8 | async-start | bytes 1585152 | tf_op jit(solution)/shard_map/all_gather | solution.py:54
  34.3 94.2 %all-gather.9.cloned.1.call-start = ((), (), s32[]{:S(2)}) async-start(), calls=%async_computation.9 | async-start | bytes 1769472 | tf_op jit(solution)/shard_map/all_gather | solution.py:54
  76.7 1.8 collective-permute-start
  86.0 64.9 %all-gather.17.cloned.1.call-start = ((), (), s32[]{:S(2)}) async-start(), calls=%async_computation.13 | async-start | bytes 1310720 | tf_op jit(solution)/shard_map/all_gather | solution.py:99
  86.7 76.6 %all-gather.13.cloned.1.call-start = ((), (), s32[]{:S(2)}) async-start(), calls=%async_computation.11 | async-start | bytes 1310720 | tf_op jit(solution)/shard_map/all_gather | solution.py:98
  87.3 121.2 %all-gather.11.cloned.1.call-start = ((), (), s32[]{:S(2)}) async-start(), calls=%async_computation.10 | async-start | bytes 1585152 | tf_op jit(solution)/shard_map/all_gather | solution.py:54
  150.8 249.0 %reduce-scatter.9.cloned.1.call-start = ((), (), s32[]{:S(2)}) async-start(), calls=%async_computation.14 | async-start | bytes 12681216 | tf_op jit(solution)/shard_map/reduce_scatter | solution.py:70
  158.0 241.8 %copy-start.42 = (f32[512]{0:T(512)S(1)}, f32[512]{0:T(512)}, u32[]{:S(2)}) copy-start(f32[512]{0:T(512)} %param.28) | copy-start | bytes 6148
  158.1 323.3 %reduce-scatter.11.cloned.1.call-start = ((), (), s32[]{:S(2)}) async-start(), calls=%async_computation.15 | async-start | bytes 3170304 | tf_op jit(solution)/shard_map/reduce_scatter | solution.py:70
  163.4 242.4 %copy-start.15 = (bf16[1024,512]{1,0:T(8,128)(2,1)S(1)}, bf16[1024,512]{1,0:T(8,128)(2,1)}, u32[]{:S(2)}) copy-start(bf16[1024,512]{1,0:T(8,128)(2,1)} %all-gather.13.cloned.1.call-done) | copy-start | bytes 3145732
  408.3 166.3 %all-gather.15.cloned.1.call-start = ((), (), s32[]{:S(2)}) async-start(), calls=%async_computation.12 | async-start | bytes 6340608 | tf_op jit(solution)/shard_map/all_gather | solution.py:54
  409.0 245.2 %reduce-scatter.13.cloned.1.call-start = ((), (), s32[]{:S(2)}) async-start(), calls=%async_computation.16 | async-start | bytes 3170304 | tf_op jit(solution)/shard_map/reduce_scatter | solution.py:70
  582.4 98.2 %reduce-scatter.21.cloned.1.call-start = ((), (), s32[]{:S(2)}) async-start(), calls=%async_computation.20 | async-start | bytes 1310720 | tf_op jit(solution)/shard_map/reduce_scatter | solution.py:215
  585.9 117.2 %reduce-scatter.19.cloned.1.call-start = ((), (), s32[]{:S(2)}) async-start(), calls=%async_computation.19 | async-start | bytes 327680 | tf_op jit(solution)/shard_map/reduce_scatter | solution.py:212
  587.3 143.0 %reduce-scatter.23.cloned.1.call-start = ((), (), s32[]{:S(2)}) async-start(), calls=%async_computation.21 | async-start | bytes 1310720 | tf_op jit(solution)/shard_map/reduce_scatter | solution.py:218
  593.5 162.6 %reduce-scatter.17.cloned.1.call-start = ((), (), s32[]{:S(2)}) async-start(), calls=%async_computation.18 | async-start | bytes 983040 | tf_op jit(solution)/shard_map/reduce_scatter | solution.py:209
  669.9 2.3 collective-permute-start.1
  675.6 157.4 %reduce-scatter.15.cloned.1.call-start = ((), (), s32[]{:S(2)}) async-start(), calls=%async_computation.17 | async-start | bytes 3170304 | tf_op jit(solution)/shard_map/reduce_scatter | solution.py:70
  678.2 176.1 %copy-start.31 = (f32[128]{0:T(128)S(1)}, f32[128]{0:T(128)}, u32[]{:S(2)}) copy-start(f32[128]{0:T(128)} %get-tuple-element.16) | copy-start | bytes 1540
  678.2 176.1 %copy-start.32 = (f32[128]{0:T(128)S(1)}, f32[128]{0:T(128)}, u32[]{:S(2)}) copy-start(f32[128]{0:T(128)} %get-tuple-element.22) | copy-start | bytes 1540
  678.2 176.1 %copy-start.33 = (f32[512]{0:T(512)S(1)}, f32[512]{0:T(512)}, u32[]{:S(2)}) copy-start(f32[512]{0:T(512)} %get-tuple-element.50) | copy-start | bytes 6148
  678.2 176.1 %copy-start.36 = (f32[128]{0:T(128)S(1)}, f32[128]{0:T(128)}, u32[]{:S(2)}) copy-start(f32[128]{0:T(128)} %get-tuple-element.28) | copy-start | bytes 1540
  678.2 176.1 %copy-start.37 = (f32[128]{0:T(128)S(1)}, f32[128]{0:T(128)}, u32[]{:S(2)}) copy-start(f32[128]{0:T(128)} %get-tuple-element.29) | copy-start | bytes 1540
  678.2 182.5 %copy-start.9 = (f32[685,128]{1,0:T(8,128)S(1)}, f32[685,128]{1,0:T(8,128)}, u32[]{:S(2)}) copy-start(f32[685,128]{1,0:T(8,128)} %copy-done.8) | copy-start | bytes 1052164
  (38 other events, 1841.7 us)
Sparse Core Ops, SparseCore 0:
  34.4 39.8 all-gather.6
  86.1 42.3 all-gather.8
  130.1 15.0 all-gather.16
  146.6 16.6 all-gather.12
  165.8 42.6 all-gather.10
  212.0 187.7 reduce-scatter.8
  408.4 72.9 reduce-scatter.10
  483.4 91.1 all-gather.14
  582.5 71.7 reduce-scatter.12
  656.6 23.8 reduce-scatter.20
  683.0 20.0 reduce-scatter.18
  705.5 24.7 reduce-scatter.22
  732.8 23.2 reduce-scatter.16
  759.5 73.5 reduce-scatter.14
where the time goes:
time: 870 us; the launch traced here: 869 us
  waiting for transfers between devices  663 us (76%)
  blocking collectives  104 us (12%)
  matrix products  56.9 us (7%)
  other arithmetic  21.6 us (2%)
  between operations  14.6 us (2%)
  local copies, waits for them, and re-layouts  9.18 us (1%)
    reduce_scatter x4, waiting for transfers between devices, back_project(): return lax.psum_scatter(term, 'gy', scatter_dimension=1, tiled=True)  400 us
    all_gather x4, waiting for transfers between devices, project(): lax.all_gather(inputs, 'gy', axis=1, tiled=True)  181 us
    psum x2, blocking collectives, norm_forward(): lax.psum((jnp.sum(rows, axis=1), jnp.sum(rows * rows, axis=1)), 'gy')  42.5 us
    psum x2, blocking collectives, norm_backward(): lax.psum((jnp.sum(scaled, axis=1), jnp.sum(scaled * normed, axis=1)), 'gy')  40.4 us
    reduce_scatter x1, waiting for transfers between devices, on_device(): lax.psum_scatter(grad_fc2.astype(jnp.bfloat16), 'gx', scatter_dimension=0...  25.7 us
    reduce_scatter x1, waiting for transfers between devices, on_device(): lax.psum_scatter(grad_qkv.astype(jnp.bfloat16), 'gx', scatter_dimension=0...  23.8 us
    reduce_scatter x1, waiting for transfers between devices, on_device(): lax.psum_scatter(grad_proj.astype(jnp.bfloat16), 'gx', scatter_dimension=...  20.8 us
  transfers between devices with their start and end apart: 16, of which 14 were waited for; matrix products, arithmetic and copies ran while one was open for 6% of the time, Pallas kernels for 0%

commit v1 on v0

--- a/solution.py
+++ b/solution.py
@@ -1,6 +1,10 @@
+import functools
+
 import jax
 import jax.numpy as jnp
 from jax import lax
+from jax.experimental import pallas as pl
+from jax.experimental.pallas import tpu as pltpu
 from jax.sharding import PartitionSpec as P
 
 D = 1024
@@ -35,39 +39,155 @@
     return normal_cdf(values) + values * jnp.exp(-0.5 * values * values) * INV_ROOT_TAU
 
 
-def norm_forward(rows, gain, shift):
-    totals, squares = lax.psum((jnp.sum(rows, axis=1), jnp.sum(rows * rows, axis=1)), "gy")
-    row_mean = totals / D
-    inv_std = lax.rsqrt(squares / D - row_mean * row_mean + EPS)[:, None]
-    normed = (rows - row_mean[:, None]) * inv_std
+def norm_full(rows, gain, shift):
+    row_mean = jnp.mean(rows, axis=1, keepdims=True)
+    inv_std = lax.rsqrt(jnp.mean(rows * rows, axis=1, keepdims=True) - row_mean * row_mean + EPS)
+    normed = (rows - row_mean) * inv_std
     return (normed, inv_std, (normed * gain + shift).astype(jnp.bfloat16))
 
 
-def norm_backward(grad_normed, normed, inv_std, gain):
-    scaled = grad_normed * gain
-    first, second = lax.psum((jnp.sum(scaled, axis=1), jnp.sum(scaled * normed, axis=1)), "gy")
-    return inv_std * (scaled - first[:, None] / D - normed * (second[:, None] / D))
-
-
-def project(inputs, weight):
-    result = jnp.dot(
-        lax.all_gather(inputs, "gy", axis=1, tiled=True), weight, preferred_element_type=jnp.float32
-    )
-    return (result, inputs)
+def gather_columns(block):
+    return lax.all_gather(block, "gy", axis=1, tiled=True)
+
+
+def ring_kernel(parts, block_ref, out_ref, send_sem, recv_sem):
+    half = parts // 2
+
+    def index_of(place):
+        back = place // half
+        return (1 - back) * (2 * place) + back * (2 * (parts - 1 - place) + 1)
+
+    me = lax.axis_index("gy")
+    odd = me % 2
+    place = (1 - odd) * (me // 2) + odd * (parts - 1 - me // 2)
+    sides = (index_of((place + 1) % parts), index_of((place + parts - 1) % parts))
+    barrier = pltpu.get_barrier_semaphore()
+    for side in sides:
+        pl.semaphore_signal(
+            barrier, inc=1, device_id={"gy": side}, device_id_type=pl.DeviceIdType.MESH
+        )
+    pl.semaphore_wait(barrier, 2)
+    copies = []
+    for step in range(half):
+        owners = (
+            index_of((place + parts - step) % parts),
+            index_of((place + step) % parts),
+        )
+        started = []
+        for way in range(2):
+            if way == 1 and step == half - 1:
+                continue
+            copy = pltpu.make_async_remote_copy(
+                src_ref=block_ref if step == 0 else out_ref.at[owners[way]],
+                dst_ref=out_ref.at[owners[way]],
+                send_sem=send_sem.at[way, step],
+                recv_sem=recv_sem.at[way, step],
+                device_id={"gy": sides[way]},
+                device_id_type=pl.DeviceIdType.MESH,
+            )
+            copy.start()
+            started.append(copy)
+        if step == 0:
+            out_ref[me] = block_ref[...]
+        for copy in started:
+            copy.wait_recv()
+        copies += started
+    for copy in copies:
+        copy.wait_send()
+
+
+def ring_columns(block, call):
+    parts = lax.axis_size("gy")
+    count, width = block.shape
+    if parts % 2 or parts < 4:
+        return gather_columns(block)
+    got = pl.pallas_call(
+        functools.partial(ring_kernel, parts),
+        out_shape=jax.ShapeDtypeStruct((parts, count, width), block.dtype),
+        in_specs=[pl.BlockSpec(memory_space=pltpu.VMEM)],
+        out_specs=pl.BlockSpec(memory_space=pltpu.VMEM),
+        scratch_shapes=[
+            pltpu.SemaphoreType.DMA((2, parts // 2)),
+            pltpu.SemaphoreType.DMA((2, parts // 2)),
+        ],
+        compiler_params=pltpu.CompilerParams(collective_id=call, has_side_effects=True),
+    )(block)
+    return jnp.transpose(got, (1, 0, 2)).reshape(count, parts * width)
+
+
+def spread_columns(block):
+    parts = lax.axis_size("gy")
+    got = lax.all_to_all(
+        jnp.broadcast_to(block[None], (parts,) + block.shape), "gy", 0, 0, tiled=True
+    )
+    return jnp.transpose(got, (1, 0, 2)).reshape(block.shape[0], parts * block.shape[1])
+
+
+def column_blocks(block):
+    parts = lax.axis_size("gy")
+    count, full = block.shape
+    return jnp.transpose(block.reshape(count, parts, full // parts), (1, 0, 2))
+
+
+def scatter_sum(blocks, axis):
+    got = lax.all_to_all(blocks, axis, 0, 0, tiled=True)
+    return jnp.sum(got.astype(jnp.float32), axis=0)
+
+
+def own_columns(block, width):
+    return lax.dynamic_slice_in_dim(block, lax.axis_index("gy") * width, width, axis=1)
+
+
+def sum_rows(term):
+    parts = lax.axis_size("gx")
+    blocks = term.reshape(parts, term.shape[0] // parts, term.shape[1])
+    return scatter_sum(blocks, "gx")
+
+
+def weight_grad_rows(saved, grad_out):
+    term = jnp.einsum("tk,tn->kn", saved, grad_out, preferred_element_type=jnp.float32)
+    return lax.psum_scatter(
+        term.astype(jnp.bfloat16), "gx", scatter_dimension=0, tiled=True
+    ).astype(jnp.float32)
 
 
 def weight_grad(saved, grad_out):
-    return jnp.einsum(
-        "tk,tn->kn",
-        lax.all_gather(saved, "gy", axis=1, tiled=True),
-        grad_out,
-        preferred_element_type=jnp.float32,
-    )
-
-
-def back_project(grad_out, weight):
+    term = jnp.einsum("tk,tn->kn", saved, grad_out, preferred_element_type=jnp.float32)
+    return sum_rows(term.astype(jnp.bfloat16))
+
+
+def lanes_of(column, width):
+    count = column.shape[0]
+    lines = -(-count // width)
+    return jnp.pad(column, (0, lines * width - count)).reshape(lines, width)
+
+
+def back_norm(grad_out, weight, normed, normed_own, inv_std, gain, gain_own):
+    parts = lax.axis_size("gy")
+    count, full = normed.shape
+    width = full // parts
     term = jnp.einsum("tn,kn->tk", grad_out, weight, preferred_element_type=jnp.float32)
-    return lax.psum_scatter(term, "gy", scatter_dimension=1, tiled=True)
+    scaled = term * gain
+    first = lanes_of(jnp.sum(scaled, axis=1), width)
+    second = lanes_of(jnp.sum(scaled * normed, axis=1), width)
+    lines = first.shape[0]
+    sums = jnp.concatenate([first, second], axis=0).astype(jnp.bfloat16)
+    blocks = column_blocks(term.astype(jnp.bfloat16))
+    sent = jnp.concatenate(
+        [blocks, jnp.broadcast_to(sums[None], (parts,) + sums.shape)], axis=1
+    )
+    back = scatter_sum(sent, "gy")
+    grad_normed = back[:count]
+    first = back[count : count + lines].reshape(-1)[:count, None]
+    second = back[count + lines :].reshape(-1)[:count, None]
+    grad_rows = inv_std * (
+        grad_normed * gain_own - first / full - normed_own * (second / full)
+    )
+    return (
+        grad_rows,
+        jnp.sum(grad_normed * normed_own, axis=0),
+        jnp.sum(grad_normed, axis=0),
+    )
 
 
 def on_device(
@@ -92,15 +212,21 @@
     half_len = count // IMGS
     heads_here = qkv_weight.shape[1] // (3 * HD)
     factor = HD ** (-0.5)
-    full_qkv, full_proj, full_fc1, full_fc2 = (
-        lax.all_gather(qkv_weight, "gx", axis=0, tiled=True),
-        lax.all_gather(proj_weight, "gx", axis=0, tiled=True),
-        lax.all_gather(fc1_weight, "gx", axis=0, tiled=True),
-        lax.all_gather(fc2_weight, "gx", axis=0, tiled=True),
-    )
-    inputs = tokens.astype(jnp.float32)
-    normed_one, inv_one, norm_one = norm_forward(inputs, norm1_gain, norm1_shift)
-    mixed, saved_one = project(norm_one, full_qkv)
+    width = tokens.shape[1]
+    full_tokens = ring_columns(tokens, 0)
+    vectors = spread_columns(
+        jnp.stack([norm1_gain, norm1_shift, proj_bias, scale_attn, norm2_gain, norm2_shift, scale_mlp])
+    )
+    gain_one, shift_one, bias_proj, full_scale_attn, gain_two, shift_two, full_scale_mlp = vectors
+    full_qkv = lax.all_gather(qkv_weight, "gx", axis=0, tiled=True)
+    all_proj = lax.all_gather(ring_columns(proj_weight, 1), "gx", axis=0, tiled=True)
+    full_fc1 = lax.all_gather(fc1_weight, "gx", axis=0, tiled=True)
+    full_fc2 = lax.all_gather(fc2_weight, "gx", axis=0, tiled=True)
+    rows_fc2 = lax.all_to_all(full_fc2, "gy", split_axis=0, concat_axis=1, tiled=True)
+    full_cotangent = gather_columns(cotangent)
+    inputs = full_tokens.astype(jnp.float32)
+    normed_one, inv_one, norm_one = norm_full(inputs, gain_one, shift_one)
+    mixed = jnp.dot(norm_one, full_qkv, preferred_element_type=jnp.float32)
     mixed = mixed.reshape(count, heads_here, 3, HD)
     biases = qv_bias.reshape(heads_here, 2, HD)
     queries = (mixed[:, :, 0] + biases[:, 0]).astype(jnp.bfloat16)
@@ -131,37 +257,54 @@
         "ihqk,ikhe->iqhe", probs, value_all, preferred_element_type=jnp.float32
     ).astype(jnp.bfloat16)
     attended = attended_img.reshape(count, heads_here * HD)
-    attn_out, saved_two = project(attended, full_proj)
-    attn_out = attn_out + proj_bias
-    middle = inputs + scale_attn * attn_out
-    normed_two, inv_two, norm_two = norm_forward(middle, norm2_gain, norm2_shift)
-    pre_act, saved_three = project(norm_two, full_fc1)
-    pre_act = pre_act + fc1_bias
+    full_attended = ring_columns(attended, 0)
+    attn_out = jnp.dot(full_attended, all_proj, preferred_element_type=jnp.float32) + bias_proj
+    middle = inputs + full_scale_attn * attn_out
+    normed_two, inv_two, norm_two = norm_full(middle, gain_two, shift_two)
+    pre_act = jnp.dot(norm_two, full_fc1, preferred_element_type=jnp.float32) + fc1_bias
     hidden = gelu_exact(pre_act).astype(jnp.bfloat16)
-    mlp_out, saved_four = project(hidden, full_fc2)
-    mlp_out = mlp_out + fc2_bias
-    output = middle + scale_mlp * mlp_out
     upstream = cotangent.astype(jnp.float32)
-    grad_scale_mlp = jnp.sum(upstream * mlp_out, axis=0)
     grad_mlp = upstream * scale_mlp
     grad_fc2_bias = jnp.sum(grad_mlp, axis=0)
-    grad_mlp_b = grad_mlp.astype(jnp.bfloat16)
-    grad_fc2 = weight_grad(saved_four, grad_mlp_b)
-    grad_hidden = back_project(grad_mlp_b, full_fc2)
+    full_grad_mlp_b = (full_cotangent.astype(jnp.float32) * full_scale_mlp).astype(jnp.bfloat16)
+    grad_hidden = jnp.einsum(
+        "tn,kn->tk", full_grad_mlp_b, rows_fc2, preferred_element_type=jnp.float32
+    )
     grad_pre = grad_hidden * gelu_slope(pre_act)
     grad_fc1_bias = jnp.sum(grad_pre, axis=0)
     grad_pre_b = grad_pre.astype(jnp.bfloat16)
-    grad_fc1 = weight_grad(saved_three, grad_pre_b)
-    grad_norm_two = back_project(grad_pre_b, full_fc1)
-    grad_gain_two = jnp.sum(grad_norm_two * normed_two, axis=0)
-    grad_shift_two = jnp.sum(grad_norm_two, axis=0)
-    grad_middle = upstream + norm_backward(grad_norm_two, normed_two, inv_two, norm2_gain)
-    grad_scale_attn = jnp.sum(grad_middle * attn_out, axis=0)
+    own_two = own_columns(normed_two, width)
+    grad_rows, grad_gain_two, grad_shift_two = back_norm(
+        grad_pre_b, full_fc1, normed_two, own_two, inv_two, gain_two, norm2_gain
+    )
+    grad_middle = upstream + grad_rows
+    grad_scale_attn = jnp.sum(grad_middle * own_columns(attn_out, width), axis=0)
     grad_attn = grad_middle * scale_attn
     grad_proj_bias = jnp.sum(grad_attn, axis=0)
     grad_attn_b = grad_attn.astype(jnp.bfloat16)
-    grad_proj = weight_grad(saved_two, grad_attn_b)
-    grad_attended = back_project(grad_attn_b, full_proj).astype(jnp.bfloat16)
+    full_grad_attn_b = ring_columns(grad_attn_b, 0)
+    own_rows_proj = lax.dynamic_slice_in_dim(
+        all_proj, lax.axis_index("gy") * width, width, axis=0
+    )
+    grad_attended = jnp.einsum(
+        "tn,kn->tk", full_grad_attn_b, own_rows_proj, preferred_element_type=jnp.float32
+    ).astype(jnp.bfloat16)
+    mlp_term = jnp.dot(hidden, rows_fc2, preferred_element_type=jnp.float32)
+    mlp_out = (
+        lax.psum_scatter(
+            column_blocks(mlp_term.astype(jnp.bfloat16)), "gy", scatter_dimension=0, tiled=False
+        ).astype(jnp.float32)
+        + fc2_bias
+    )
+    output = own_columns(middle, width) + scale_mlp * mlp_out
+    grad_scale_mlp = jnp.sum(upstream * mlp_out, axis=0)
+    fc2_term = jnp.einsum(
+        "tk,tn->kn", hidden, full_grad_mlp_b, preferred_element_type=jnp.float32
+    )
+    fc2_blocks = lax.all_to_all(column_blocks(fc2_term.astype(jnp.bfloat16)), "gy", 0, 0, tiled=True)
+    grad_fc2 = sum_rows(fc2_blocks.reshape(-1, width))
+    grad_fc1 = weight_grad_rows(norm_two, grad_pre_b)
+    grad_proj = weight_grad_rows(full_attended, grad_attn_b)
     grad_att_img = grad_attended.reshape(IMGS, half_len, heads_here, HD)
     recomputed = jnp.exp(scores - log_total)
     probs_b = recomputed.astype(jnp.bfloat16)
@@ -200,25 +343,12 @@
         .astype(jnp.bfloat16)
         .reshape(count, heads_here * 3 * HD)
     )
-    grad_qkv = weight_grad(saved_one, grad_mixed)
-    grad_norm_one = back_project(grad_mixed, full_qkv)
-    grad_gain_one = jnp.sum(grad_norm_one * normed_one, axis=0)
-    grad_shift_one = jnp.sum(grad_norm_one, axis=0)
-    grad_input = grad_middle + norm_backward(grad_norm_one, normed_one, inv_one, norm1_gain)
-    grad_qkv, grad_proj, grad_fc1, grad_fc2 = (
-        lax.psum_scatter(
-            grad_qkv.astype(jnp.bfloat16), "gx", scatter_dimension=0, tiled=True
-        ).astype(jnp.float32),
-        lax.psum_scatter(
-            grad_proj.astype(jnp.bfloat16), "gx", scatter_dimension=0, tiled=True
-        ).astype(jnp.float32),
-        lax.psum_scatter(
-            grad_fc1.astype(jnp.bfloat16), "gx", scatter_dimension=0, tiled=True
-        ).astype(jnp.float32),
-        lax.psum_scatter(
-            grad_fc2.astype(jnp.bfloat16), "gx", scatter_dimension=0, tiled=True
-        ).astype(jnp.float32),
-    )
+    grad_qkv = weight_grad(norm_one, grad_mixed)
+    own_one = own_columns(normed_one, width)
+    grad_rows, grad_gain_one, grad_shift_one = back_norm(
+        grad_mixed, full_qkv, normed_one, own_one, inv_one, gain_one, norm1_gain
+    )
+    grad_input = grad_middle + grad_rows
     smalls = lax.psum(
         (
             grad_gain_one,

time: 870 us -> 380 us (0.44)
  waiting for transfers between devices: 663 us -> 104 us
  Pallas kernels: 0 us -> 102 us
  blocking collectives: 104 us -> 17.4 us
  starting transfers between devices: 0.71 us -> 32.4 us
  local copies, waits for them, and re-layouts: 9.18 us -> 32.9 us
    reduce_scatter x8 -> x3, waiting for transfers between devices: 472 us -> 32.8 us  [the longest x2 18.7 us: weight_grad_rows(): lax.psum_scatter(term.astype(jnp.bfloat16), 'gx', scatter_dimension=0, ti...]
    all_gather x6 -> x4, waiting for transfers between devices: 187 us -> 0.04 us  [the longest x1 0.02 us: on_device(): full_fc2 = lax.all_gather(fc2_weight, 'gx', axis=0, tiled=True)]
    pallas_call x0 -> x4, Pallas kernels: none -> 102 us  [ring_columns(): pl.pallas_call(functools.partial(ring_kernel, parts), out_shape=jax.Shape...]
    psum x4 -> x0, blocking collectives: 82.9 us -> none  [the longest x2 42.5 us: norm_forward(): lax.psum((jnp.sum(rows, axis=1), jnp.sum(rows * rows, axis=1)), 'gy')]
    all_to_all x0 -> x7, waiting for transfers between devices: none -> 69.9 us  [the longest x4 44.2 us: scatter_sum(): got = lax.all_to_all(blocks, axis, 0, 0, tiled=True)]
    all_to_all x0 -> x7, starting transfers between devices: none -> 32 us  [the longest x4 15.9 us: scatter_sum(): got = lax.all_to_all(blocks, axis, 0, 0, tiled=True)]
  transfers between devices with their start and end apart: 16 -> 16, of which waited for: 14 -> 7; matrix products, arithmetic and copies ran while one was open for 6% -> 26% of each run, Pallas kernels for 0% -> 27%
where the time goes in v1:
time: 380 us; the launch traced here: 379 us
  waiting for transfers between devices  104 us (27%)
  Pallas kernels  102 us (27%)
  matrix products  49 us (13%)
  local copies, waits for them, and re-layouts  32.9 us (9%)
  starting transfers between devices  32.4 us (9%)
  other arithmetic  26.1 us (7%)
  blocking collectives  17.4 us (5%)
  between operations  15.3 us (4%)
    pallas_call x4, Pallas kernels, ring_columns(): pl.pallas_call(functools.partial(ring_kernel, parts), out_shape=jax.Shape...  102 us
    all_to_all x4, waiting for transfers between devices, scatter_sum(): got = lax.all_to_all(blocks, axis, 0, 0, tiled=True)  44.2 us
    reduce_scatter x2, waiting for transfers between devices, weight_grad_rows(): lax.psum_scatter(term.astype(jnp.bfloat16), 'gx', scatter_dimension=0, ti...  18.7 us
    all_to_all x1, waiting for transfers between devices, on_device(): lax.all_to_all(column_blocks(fc2_term.astype(jnp.bfloat16)), 'gy', 0, 0,...  17.9 us
    all_to_all x4, starting transfers between devices, scatter_sum(): got = lax.all_to_all(blocks, axis, 0, 0, tiled=True)  15.9 us
    reduce_scatter x1, waiting for transfers between devices, on_device(): lax.psum_scatter(column_blocks(mlp_term.astype(jnp.bfloat16)), 'gy', scat...  14.2 us
    unnamed x125, local copies, waits for them, and re-layouts  13.4 us
    all_gather x1, blocking collectives, on_device(): full_qkv = lax.all_gather(qkv_weight, 'gx', axis=0, tiled=True)  11 us
  transfers between devices with their start and end apart: 16, of which 7 were waited for; matrix products, arithmetic and copies ran while one was open for 26% of the time, Pallas kernels for 27%

profile of v1, /device:TPU:0, one launch (start us, length us, event | category | flops | bytes accessed | tf_op | source)
XLA Modules:
  0.0 379.0 jit_solution(2521226600019703338)
XLA Ops:
  8.1 19.1 %shard_map.281 = bf16[8,256,128]{2,1,0:T(8,128)(2,1)} custom-call(bf16[256,128]{1,0:T(8,128)(2,1)} %block_ref.3), custom_call_target="tpu_custom_call" | custom-call | tf_op jit(solution)/shard_map/pallas_call | solution.py:104
  29.9 4.3 %all-to-all-start = ((f32[8,7,128]{2,1,0:T(8,128)}), f32[8,7,128]{2,1,0:T(8,128)S(1)}, u32[]{:S(2)}, u32[]{:S(2)}) async-start(f32[8,7,128]{2,1,0:T(8,128)} %broadcast_in_dim.6), calls=%async_computation | async-start | bytes 65536 | tf_op jit(solution)/shard_map/all_to_all | solution.py:120
  35.1 11.0 %all_gather.15 = bf16[1024,384]{1,0:T(8,128)(2,1)S(1)} all-gather(bf16[256,384]{1,0:T(8,128)(2,1)S(1)} %copy-done.23), channel_id=1, replica_groups=mesh['gx'=4,'gy'=8] {'gx'}, dimensions={0}, use_global_device_ids=true | all-gather | bytes 983040 | tf_op jit(solution)/shard_map/all_gather | solution.py:221
  46.2 25.8 %shard_map.279 = bf16[8,685,128]{2,1,0:T(8,128)(2,1)} custom-call(bf16[685,128]{1,0:T(8,128)(2,1)} %block_ref.2), custom_call_target="tpu_custom_call" | custom-call | tf_op jit(solution)/shard_map/pallas_call | solution.py:104
  95.5 31.9 %shard_map.280 = bf16[8,685,128]{2,1,0:T(8,128)(2,1)} custom-call(bf16[685,128]{1,0:T(8,128)(2,1)} %copy.73.block_ref), custom_call_target="tpu_custom_call" | custom-call | tf_op jit(solution)/shard_map/pallas_call | solution.py:104
  129.7 7.6 %all-to-all-start.1 = ((bf16[8,512,128]{2,1,0:T(8,128)(2,1)}), bf16[8,512,128]{2,1,0:T(8,128)(2,1)}, u32[]{:S(2)}, u32[]{:S(2)}) async-start(bf16[8,512,128]{2,1,0:T(8,128)(2,1)} %bitcast.229), calls=%async_computation.1 | async-start | bytes 2097152 | tf_op jit(solution)/shard_map/all_to_all | solution.py:225
  137.3 5.9 %fusion.52 = (f32[685]{0:T(1024)S(1)}, f32[685]{0:T(1024)S(1)}, f32[685,1024]{1,0:T(8,128)S(1)}, f32[685,1024]{1,0:T(8,128)}) fusion(f32[685,1024]{1,0:T(8,128)} %bitcast.189, f32[1024]{0:T(1024)S(1)} %bitcast.255, f32[1024]{0:T(1024)S(1)} %bitcast.254, bf16[685,1024]{1,0:T(8,128)(2,1)S(1)} %bitcast.201, bf16[1024,1024]{0,1:T(8,128)(2,1)} %all-gather.5.cloned.1.call-done), kind=kOutput, calls=%fused_computation.137 | convolution fusion | flops 1440756480 | bytes 11930984 | tf_op jit(solution)/shard_map/dot_general | solution.py:261
  146.7 4.2 %multiply_convert_fusion.2 = (bf16[685,512]{1,0:T(8,128)(2,1)S(1)}, f32[685,512]{1,0:T(8,128)}) fusion(f32[512]{0:T(512)S(1)} %copy-done.51, bf16[1024,512]{1,0:T(8,128)(2,1)} %all-gather.7.cloned.1.call-done, f32[685,1024]{1,0:T(8,128)} %subtract_multiply_fusion.1, f32[1024]{0:T(1024)S(1)} %bitcast.247, f32[1024]{0:T(1024)S(1)} %bitcast.249), kind=kOutput, calls=%fused_computation.56 | convolution fusion | flops 722483200 | bytes 5968896 | tf_op jit(solution)/shard_map/dot_general | solution.py:264
  154.7 7.8 %all-to-all-done.1 = bf16[8,512,128]{2,1,0:T(8,128)(2,1)} async-done(((bf16[8,512,128]{2,1,0:T(8,128)(2,1)}), bf16[8,512,128]{2,1,0:T(8,128)(2,1)}, u32[]{:S(2)}, u32[]{:S(2)}) %all-to-all-start.1) | async-done | bytes 1048608 | tf_op jit(solution)/shard_map/all_to_all | solution.py:225
  162.5 4.2 %all-to-all-start.5 = ((bf16[8,512,128]{2,1,0:T(8,128)(2,1)}), bf16[8,512,128]{2,1,0:T(8,128)(2,1)}, u32[]{:S(2)}, u32[]{:S(2)}) async-start(bf16[8,512,128]{2,1,0:T(8,128)(2,1)} %bitcast.186), calls=%async_computation.8 | async-start | bytes 2097152 | tf_op jit(solution)/shard_map/all_to_all | solution.py:304
  172.2 3.8 %fusion.55 = (f32[512]{0:T(512)}, bf16[685,512]{1,0:T(8,128)(2,1)S(1)}) fusion(f32[685,512]{1,0:T(8,128)} %get-tuple-element.79, bf16[512,1024]{0,1:T(8,128)(2,1)S(1)} %bitcast.231, bf16[685,1024]{1,0:T(8,128)(2,1)} %all-gather.11.cloned.1.call-done, f32[1024]{0:T(1024)S(1)} %bitcast.253), kind=kOutput, calls=%fused_computation.140 | convolution fusion | flops 724236288 | bytes 4561920 | tf_op jit(solution)/shard_map/tn,kn->tk/dot_general | solution.py:270
  179.1 17.9 %all-to-all-done.5 = bf16[8,512,128]{2,1,0:T(8,128)(2,1)} async-done(((bf16[8,512,128]{2,1,0:T(8,128)(2,1)}), bf16[8,512,128]{2,1,0:T(8,128)(2,1)}, u32[]{:S(2)}, u32[]{:S(2)}) %all-to-all-start.5) | async-done | bytes 1048608 | tf_op jit(solution)/shard_map/all_to_all | solution.py:304
  205.2 32.6 %all-to-all-done.2 = bf16[8,697,128]{2,1,0:T(8,128)(2,1)S(1)} async-done(((bf16[8,697,128]{2,1,0:T(8,128)(2,1)}), bf16[8,697,128]{2,1,0:T(8,128)(2,1)S(1)}, u32[]{:S(2)}, u32[]{:S(2)}) %all-to-all-start.2) | async-done | bytes 1427488 | tf_op jit(solution)/shard_map/all_to_all | solution.py:133
  237.8 4.5 %all-to-all-start.6 = ((bf16[4,1024,128]{2,1,0:T(8,128)(2,1)}), bf16[4,1024,128]{2,1,0:T(8,128)(2,1)}, u32[]{:S(2)}, u32[]{:S(2)}) async-start(bf16[4,1024,128]{2,1,0:T(8,128)(2,1)} %bitcast.76), calls=%async_computation.9 | async-start | bytes 2097152 | tf_op jit(solution)/shard_map/all_to_all | solution.py:133
  242.5 14.2 %reduce-scatter.4.cloned.1.call-done = bf16[1,685,128]{2,1,0:T(8,128)(2,1)} async-done(((bf16[8,685,128]{2,1,0:T(8,128)(2,1)}), bf16[1,685,128]{2,1,0:T(8,128)(2,1)}) %reduce-scatter.4.cloned.1.call-update) | async-done | bytes 175376 | tf_op jit(solution)/shard_map/reduce_scatter | solution.py:294
  260.9 24.9 %shard_map.282 = bf16[8,685,128]{2,1,0:T(8,128)(2,1)} custom-call(bf16[685,128]{1,0:T(8,128)(2,1)} %multiply_convert_fusion.5.block_ref), custom_call_target="tpu_custom_call" | custom-call | tf_op jit(solution)/shard_map/pallas_call | solution.py:104
  295.1 4.8 %fusion.10 = f32[1,1370,2,64]{1,3,2,0:T(8,128)S(1)} fusion(bf16[685,2,64]{0,2,1:T(8,128)(2,1)} %bitcast.222, f32[2,685,1370]{2,1,0:T(8,128)} %copy-done, f32[2,685]{1,0:T(2,128)} %log_add_fusion), kind=kOutput, calls=%fused_computation.31 | convolution fusion | flops 245873904 | bytes 8389880 | tf_op jit(solution)/shard_map/ihqk,iqhe->ikhe/dot_general | solution.py:311
  309.9 4.2 %all-to-all-start.4 = ((bf16[4,256,384]{2,1,0:T(8,128)(2,1)}), bf16[4,256,384]{2,1,0:T(8,128)(2,1)}, u32[]{:S(2)}, u32[]{:S(2)}) async-start(bf16[4,256,384]{2,1,0:T(8,128)(2,1)} %bitcast.232), calls=%async_computation.5 | async-start | bytes 1572864 | tf_op jit(solution)/shard_map/all_to_all | solution.py:133
  314.1 4.0 %multiply_reduce_fusion.4 = (bf16[685]{0:T(1024)(128)(2,1)S(1)}, bf16[685]{0:T(1024)(128)(2,1)S(1)}, f32[685,1024]{1,0:T(8,128)}, bf16[685,1024]{1,0:T(8,128)(2,1)S(1)}) fusion(f32[1024]{0:T(1024)S(1)} %bitcast.239, f32[685]{0:T(1024)S(1)} %copy-done.25, f32[685,1024]{1,0:T(8,128)S(1)} %bitcast.190, f32[685]{0:T(1024)S(1)} %copy-done.30, ...), kind=kOutput, calls=%fused_computation.28 | convolution fusion | flops 543614592 | bytes 8339228 | tf_op jit(solution)/shard_map/tn,kn->tk/dot_general | solution.py:169
  320.2 5.6 %all-to-all-done.4 = bf16[4,256,384]{2,1,0:T(8,128)(2,1)} async-done(((bf16[4,256,384]{2,1,0:T(8,128)(2,1)}), bf16[4,256,384]{2,1,0:T(8,128)(2,1)}, u32[]{:S(2)}, u32[]{:S(2)}) %all-to-all-start.4) | async-done | bytes 786464 | tf_op jit(solution)/shard_map/all_to_all | solution.py:133
  325.8 3.6 all-to-all-start.3
  335.1 18.7 %reduce-scatter.6.cloned.1.call-done = bf16[256,128]{1,0:T(8,128)(2,1)} async-done(((bf16[1024,128]{1,0:T(8,128)(2,1)}), bf16[256,128]{1,0:T(8,128)(2,1)}) %reduce-scatter.6.cloned.1.call-update) | async-done | bytes 65552 | tf_op jit(solution)/shard_map/reduce_scatter | solution.py:149
  357.4 6.0 %all-to-all-done.3 = bf16[8,697,128]{2,1,0:T(8,128)(2,1)S(1)} async-done(((bf16[8,697,128]{2,1,0:T(8,128)(2,1)}), bf16[8,697,128]{2,1,0:T(8,128)(2,1)S(1)}, u32[]{:S(2)}, u32[]{:S(2)}) %all-to-all-start.3) | async-done | bytes 1427488 | tf_op jit(solution)/shard_map/all_to_all | solution.py:133
  365.8 6.3 %all-reduce.4 = (f32[128]{0:T(128)}, f32[128]{0:T(128)}, f32[256]{0:T(256)}, f32[128]{0:T(128)}, f32[128]{0:T(128)}, /*index=5*/f32[128]{0:T(128)}, f32[128]{0:T(128)}, f32[512]{0:T(512)}, f32[128]{0:T(128)}, f32[128]{0:T(128)}) all-reduce(f32[128]{0:T(128)S(1)} %get-tuple-element.27, ...), channel_id=1, replica_groups=mesh['gx'=4,'gy'=8] {'gx'}, use_global_device_ids=true, to_apply=%region_15.16 | all-reduce | flops 1792 | bytes 14336 | tf_op jit(solution)/shard_map/psum | solution.py:352
  (233 shorter events, 90.7 us)
Async XLA Ops:
  7.3 27.8 %copy-start.45 = (f32[256]{0:T(256)S(1)}, f32[256]{0:T(256)}, u32[]{:S(2)}) copy-start(f32[256]{0:T(256)} %param.21) | copy-start | bytes 3076
  7.3 27.9 %copy-start.23 = (bf16[256,384]{1,0:T(8,128)(2,1)S(1)}, bf16[256,384]{1,0:T(8,128)(2,1)}, u32[]{:S(2)}) copy-start(bf16[256,384]{1,0:T(8,128)(2,1)} %param.20) | copy-start | bytes 589828
  7.3 122.5 %all-gather.9.cloned.1.call-start = ((), (), s32[]{:S(2)}) async-start(), calls=%async_computation.12 | async-start | bytes 1310720 | tf_op jit(solution)/shard_map/all_gather | solution.py:224
  8.0 129.3 %all-gather.5.cloned.1.call-start = ((), (), s32[]{:S(2)}) async-start(), calls=%async_computation.10 | async-start | bytes 2621440 | tf_op jit(solution)/shard_map/all_gather | solution.py:222
  29.9 45.2 %all-to-all-start = ((f32[8,7,128]{2,1,0:T(8,128)}), f32[8,7,128]{2,1,0:T(8,128)S(1)}, u32[]{:S(2)}, u32[]{:S(2)}) async-start(f32[8,7,128]{2,1,0:T(8,128)} %broadcast_in_dim.6), calls=%async_computation | async-start | bytes 65536 | tf_op jit(solution)/shard_map/all_to_all | solution.py:120
  34.3 112.4 %all-gather.7.cloned.1.call-start = ((), (), s32[]{:S(2)}) async-start(), calls=%async_computation.11 | async-start | bytes 1310720 | tf_op jit(solution)/shard_map/all_gather | solution.py:223
  35.0 115.9 %all-gather.11.cloned.1.call-start = ((), (), s32[]{:S(2)}) async-start(), calls=%async_computation.14 | async-start | bytes 1585152 | tf_op jit(solution)/shard_map/all_gather | solution.py:50
  46.2 29.0 %copy-start.3 = (bf16[1024,384]{1,0:T(8,128)(2,1)}, bf16[1024,384]{1,0:T(8,128)(2,1)S(1)}, u32[]{:S(2)}) copy-start(bf16[1024,384]{1,0:T(8,128)(2,1)S(1)} %all_gather.15) | copy-start | bytes 2359300
  82.1 3.7 collective-permute-start
  94.7 34.5 %copy-start.21 = (bf16[2,64,685]{2,1,0:T(8,128)(2,1)}, bf16[2,64,685]{2,1,0:T(8,128)(2,1)S(1)}, u32[]{:S(2)}) copy-start(bf16[2,64,685]{2,1,0:T(8,128)(2,1)S(1)} %fusion.22) | copy-start | bytes 526084
  129.7 32.7 %all-to-all-start.1 = ((bf16[8,512,128]{2,1,0:T(8,128)(2,1)}), bf16[8,512,128]{2,1,0:T(8,128)(2,1)}, u32[]{:S(2)}, u32[]{:S(2)}) async-start(bf16[8,512,128]{2,1,0:T(8,128)(2,1)} %bitcast.229), calls=%async_computation.1 | async-start | bytes 2097152 | tf_op jit(solution)/shard_map/all_to_all | solution.py:225
  162.5 34.5 %all-to-all-start.5 = ((bf16[8,512,128]{2,1,0:T(8,128)(2,1)}), bf16[8,512,128]{2,1,0:T(8,128)(2,1)}, u32[]{:S(2)}, u32[]{:S(2)}) async-start(bf16[8,512,128]{2,1,0:T(8,128)(2,1)} %bitcast.186), calls=%async_computation.8 | async-start | bytes 2097152 | tf_op jit(solution)/shard_map/all_to_all | solution.py:304
  166.7 89.9 %reduce-scatter.4.cloned.1.call-start = ((), (), s32[]{:S(2)}) async-start(), calls=%async_computation.13 | async-start | bytes 1585152 | tf_op jit(solution)/shard_map/reduce_scatter | solution.py:294
  196.9 40.8 %all-to-all-start.2 = ((bf16[8,697,128]{2,1,0:T(8,128)(2,1)}), bf16[8,697,128]{2,1,0:T(8,128)(2,1)S(1)}, u32[]{:S(2)}, u32[]{:S(2)}) async-start(bf16[8,697,128]{2,1,0:T(8,128)(2,1)} %pad_maximum_fusion), calls=%async_computation.3 | async-start | bytes 2883584 | tf_op jit(solution)/shard_map/all_to_all | solution.py:133
  200.5 130.3 %reduce-scatter.8.cloned.1.call-start = ((), (), s32[]{:S(2)}) async-start(), calls=%async_computation.16 | async-start | bytes 1310720 | tf_op jit(solution)/shard_map/reduce_scatter | solution.py:149
  205.2 51.5 %copy-start.22 = (bf16[685,128]{1,0:T(8,128)(2,1)S(1)}, bf16[685,128]{1,0:T(8,128)(2,1)}, u32[]{:S(2)}) copy-start(bf16[685,128]{1,0:T(8,128)(2,1)} %param.17) | copy-start | bytes 526084
  205.2 51.5 %copy-start.46 = (f32[128]{0:T(128)S(1)}, f32[128]{0:T(128)}, u32[]{:S(2)}) copy-start(f32[128]{0:T(128)} %param.30) | copy-start | bytes 1540
  237.8 72.1 %all-to-all-start.6 = ((bf16[4,1024,128]{2,1,0:T(8,128)(2,1)}), bf16[4,1024,128]{2,1,0:T(8,128)(2,1)}, u32[]{:S(2)}, u32[]{:S(2)}) async-start(bf16[4,1024,128]{2,1,0:T(8,128)(2,1)} %bitcast.76), calls=%async_computation.9 | async-start | bytes 2097152 | tf_op jit(solution)/shard_map/all_to_all | solution.py:133
  304.5 1.8 collective-permute-start.1
  309.9 15.9 %all-to-all-start.4 = ((bf16[4,256,384]{2,1,0:T(8,128)(2,1)}), bf16[4,256,384]{2,1,0:T(8,128)(2,1)}, u32[]{:S(2)}, u32[]{:S(2)}) async-start(bf16[4,256,384]{2,1,0:T(8,128)(2,1)} %bitcast.232), calls=%async_computation.5 | async-start | bytes 1572864 | tf_op jit(solution)/shard_map/all_to_all | solution.py:133
  325.8 37.7 %all-to-all-start.3 = ((bf16[8,697,128]{2,1,0:T(8,128)(2,1)}), bf16[8,697,128]{2,1,0:T(8,128)(2,1)S(1)}, u32[]{:S(2)}, u32[]{:S(2)}) async-start(bf16[8,697,128]{2,1,0:T(8,128)(2,1)} %pad_maximum_fusion.1), calls=%async_computation.4 | async-start | bytes 2883584 | tf_op jit(solution)/shard_map/all_to_all | solution.py:133
  329.4 24.4 %reduce-scatter.6.cloned.1.call-start = ((), (), s32[]{:S(2)}) async-start(), calls=%async_computation.15 | async-start | bytes 327680 | tf_op jit(solution)/shard_map/reduce_scatter | solution.py:149
  334.9 28.7 %copy-start.16 = (f32[685,128]{1,0:T(8,128)S(1)}, f32[685,128]{1,0:T(8,128)}, u32[]{:S(2)}) copy-start(f32[685,128]{1,0:T(8,128)} %copy-done.15) | copy-start | bytes 1052164
  334.9 28.8 %copy-start.43 = (f32[128]{0:T(128)S(1)}, f32[128]{0:T(128)}, u32[]{:S(2)}) copy-start(f32[128]{0:T(128)} %param.18) | copy-start | bytes 1540
  (49 other events, 383.4 us)
Sparse Core Ops, SparseCore 0:
  9.6 19.4 all-gather.8
  31.2 24.5 all-gather.4
  57.4 17.1 all-gather.6
  82.3 46.9 all-gather.10
  172.3 84.3 reduce-scatter.3
  259.0 23.4 reduce-scatter.7
  333.2 20.5 reduce-scatter.5
